TPU v7x, 256 devices: a whole 4x4x8 slice. The times are simulated.
256 devices in a mesh: blk: 32 (over x_hi, z, core), req: 8 (over y, x_lo).
Axes of the slice: x: 4 (x_hi: 2, x_lo: 2; x = x_hi * 2 + x_lo), y: 4, z: 8, core: 2. Of those that a mesh axis runs over, the one named last changes fastest.
Arguments:
- prefill_queries: bfloat16 [8, 512, 1024], P('req', 'blk'), may hold values from -6 to 6
- decode_queries: bfloat16 [128, 1024], P('req'), may hold values from -6 to 6
- new_prefill: bfloat16 [8, 512, 512], P('req', 'blk'), may hold values from -6 to 6
- new_decode: bfloat16 [128, 512], P('req'), may hold values from -6 to 6
- prefill_cache: bfloat16 [8, 4096, 512], P('req', 'blk'), may hold values from -5 to 5
- decode_cache: bfloat16 [128, 4096, 512], P('req', 'blk'), may hold values from -5 to 5
- prefill_offsets: int32 [8], P('req'), may hold values from 2 to 3584, as said below
- decode_lengths: int32 [128], P('req'), may hold values from 2 to 4095, as said below
- dealing: int32 [136], replicated, may hold values from 0 to 127, as said below
Outputs:
- prefill_out: bfloat16 [8, 512, 1024], P('req', 'blk')
- decode_out: bfloat16 [128, 1024], P('req')
- prefill_cache_out: bfloat16 [8, 4096, 512], P('req', 'blk')
- decode_cache_out: bfloat16 [128, 4096, 512], P('req', 'blk')
Inputs may be any that keep to these rules, and one draw needn't show every extreme that they name: The block of prefill slot i fills positions prefill_offsets[i] to prefill_offsets[i] + 511; some slot has offset 4096 - 512. The new token of decode slot j goes to position decode_lengths[j]; some slot has length 4095. `dealing`: the first 8 entries are a permutation of 0 to 7, the other 128 a permutation of 0 to 127.
All inputs are finite; a program needn't handle non-finite values.
Results may differ from a plain program's by a relative error of at most 0.0085.
Values may be sent and summed in bfloat16 or wider, within the bound.
A program may use at most 64 MiB of HBM per device.

v0:
```python
import jax
import jax.numpy as jnp
from jax import lax
from jax.sharding import PartitionSpec as P

QUERY_HEADS = 8
KEY_VALUE_HEADS = 2
HEAD_SIZE = 128


masked_fill = -1e30


def merged(part, axis, combine):
    gathered = jax.tree.map(lambda a: lax.all_gather(a, axis), part)

    def take(source):
        return jax.tree.map(lambda a: lax.dynamic_index_in_dim(a, source, 0, False), gathered)

    return lax.fori_loop(
        1, lax.axis_size(axis), lambda source, state: combine(state, take(source)), take(0)
    )


def write_block(cache_table, block_rows, offsets, positions):
    piece_len = block_rows.shape[1]
    relative = positions[None, :] - offsets[:, None]
    picked = jax.vmap(lambda source_rows, row_index: source_rows[row_index])(
        block_rows, jnp.clip(relative, 0, piece_len - 1)
    )
    inside = (relative >= 0) & (relative < piece_len)
    return jnp.where(inside[:, :, None], picked, cache_table)


def scores_of(query_rows, cache_table, limits, key_pos):
    slot_total, row_total = (query_rows.shape[0], query_rows.shape[1])
    column_total = cache_table.shape[1]
    grouped_queries = query_rows.reshape(
        slot_total, row_total, KEY_VALUE_HEADS, QUERY_HEADS // KEY_VALUE_HEADS, HEAD_SIZE
    )
    key_portion = cache_table[:, :, : KEY_VALUE_HEADS * HEAD_SIZE].reshape(
        slot_total, column_total, KEY_VALUE_HEADS, HEAD_SIZE
    )
    scores = jnp.einsum(
        "nrgqd,ncgd->ngqrc", grouped_queries, key_portion, preferred_element_type=jnp.float32
    ) * HEAD_SIZE ** (-0.5)
    visible = (key_pos[None, None, :] <= limits[:, :, None])[:, None, None]
    return (jnp.where(visible, scores, masked_fill), visible)


def weigh_values(scores, visible, maxima, cache_table):
    slot_total, column_total = (cache_table.shape[0], cache_table.shape[1])
    exponent = jnp.where(visible, jnp.exp(scores - maxima[..., None]), 0.0)
    value_portion = cache_table[:, :, KEY_VALUE_HEADS * HEAD_SIZE :].reshape(
        slot_total, column_total, KEY_VALUE_HEADS, HEAD_SIZE
    )
    weighted = jnp.einsum(
        "ngqrc,ncgd->ngqrd",
        exponent.astype(jnp.bfloat16),
        value_portion,
        preferred_element_type=jnp.float32,
    )
    return (jnp.sum(exponent, axis=-1), weighted)


def finish_rows(totals, weighted):
    normed = weighted / totals[..., None]
    slot_total, row_total = (normed.shape[0], normed.shape[3])
    return (
        jnp.transpose(normed, (0, 3, 1, 2, 4))
        .reshape(slot_total, row_total, QUERY_HEADS * HEAD_SIZE)
        .astype(jnp.bfloat16)
    )


def combine(first, second):
    first_max, first_total, first_sum = first
    second_max, second_total, second_sum = second
    joined = jnp.maximum(first_max, second_max)
    first_scale = jnp.exp(first_max - joined)
    second_scale = jnp.exp(second_max - joined)
    return (
        joined,
        first_total * first_scale + second_total * second_scale,
        first_sum * first_scale[..., None] + second_sum * second_scale[..., None],
    )


def per_device(
    prefill_queries,
    decode_queries,
    new_prefill,
    new_decode,
    prefill_cache,
    decode_cache,
    prefill_offsets,
    decode_lengths,
    dealing,
):
    ctx_dev = prefill_cache.shape[1]
    blk_index = lax.axis_index("blk")
    positions = blk_index * ctx_dev + jnp.arange(ctx_dev, dtype=jnp.int32)
    written = positions[None, :] == decode_lengths[:, None]
    decode_cache_out = jnp.where(written[:, :, None], new_decode[:, None, :], decode_cache)
    dec_scores, dec_visible = scores_of(
        decode_queries[:, None, :], decode_cache_out, decode_lengths[:, None], positions
    )
    dec_max = jnp.max(dec_scores, axis=-1)
    dec_total, dec_sum = weigh_values(dec_scores, dec_visible, dec_max, decode_cache_out)
    dec_max, dec_total, dec_sum = merged((dec_max, dec_total, dec_sum), "blk", combine)
    decode_attn = finish_rows(dec_total, dec_sum)[:, 0, :]
    block_rows, whole_queries = (
        lax.all_gather(new_prefill, "blk", axis=1, tiled=True),
        lax.all_gather(prefill_queries, "blk", axis=1, tiled=True),
    )
    prefill_cache_out = write_block(prefill_cache, block_rows, prefill_offsets, positions)
    limits = prefill_offsets[:, None] + jnp.arange(whole_queries.shape[1], dtype=jnp.int32)[None, :]
    scores, visible = scores_of(whole_queries, prefill_cache_out, limits, positions)
    maxima = jnp.max(scores, axis=-1)
    totals, weighted = weigh_values(scores, visible, maxima, prefill_cache_out)
    peer_max, peer_total, peer_sum = (
        lax.all_to_all(maxima[None], "blk", split_axis=4, concat_axis=0, tiled=True),
        lax.all_to_all(totals[None], "blk", split_axis=4, concat_axis=0, tiled=True),
        lax.all_to_all(weighted[None], "blk", split_axis=4, concat_axis=0, tiled=True),
    )
    joined = jnp.max(peer_max, axis=0)
    peer_scale = jnp.exp(peer_max - joined[None])
    totals = jnp.sum(peer_total * peer_scale, axis=0)
    weighted = jnp.sum(peer_sum * peer_scale[..., None], axis=0)
    prefill_attn = finish_rows(totals, weighted)
    gathered_pre, gathered_dec = (
        lax.all_gather(prefill_attn, "req", axis=0, tiled=True),
        lax.all_gather(decode_attn, "req", axis=0, tiled=True),
    )
    group_index = lax.axis_index("req")
    pre_count = prefill_attn.shape[0]
    dec_count = decode_attn.shape[0]
    total_pre = gathered_pre.shape[0]
    own_pre = group_index * pre_count + jnp.arange(pre_count, dtype=jnp.int32)
    own_dec = group_index * dec_count + jnp.arange(dec_count, dtype=jnp.int32)
    pre_selector = (dealing[:total_pre][None, :] == own_pre[:, None]).astype(jnp.bfloat16)
    dec_selector = (dealing[total_pre:][None, :] == own_dec[:, None]).astype(jnp.bfloat16)
    prefill_out = jnp.einsum(
        "rs,sbf->rbf", pre_selector, gathered_pre, preferred_element_type=jnp.float32
    ).astype(jnp.bfloat16)
    decode_out = jnp.dot(dec_selector, gathered_dec, preferred_element_type=jnp.float32).astype(
        jnp.bfloat16
    )
    return (prefill_out, decode_out, prefill_cache_out, decode_cache_out)


def solution(mesh):
    in_specs = (
        P("req", "blk", None),
        P("req", None),
        P("req", "blk", None),
        P("req", None),
        P("req", "blk", None),
        P("req", "blk", None),
        P("req"),
        P("req"),
        P(),
    )
    out_specs = (
        P("req", "blk", None),
        P("req", None),
        P("req", "blk", None),
        P("req", "blk", None),
    )
    return jax.shard_map(
        per_device, mesh=mesh, in_specs=in_specs, out_specs=out_specs, check_vma=False
    )
```

profile of v0, /device:TPU:6, one launch (start us, length us, event | category | flops | bytes accessed | tf_op | source)
XLA Modules:
  0.0 344.9 jit_solution(14435808164075506)
XLA Ops:
  8.0 3.9 %copy.83 = bf16[16,128,512]{1,2,0:T(8,128)(2,1)} copy(bf16[16,128,512]{2,1,0:T(8,128)(2,1)} %param.16) | data formatting | bytes 4194304 | tf_op args[5]
  12.0 2.5 broadcast_select_fusion
  15.1 1.3 fusion.28
  16.5 2.6 copy.95
  19.8 44.6 %all_gather.30 = bf16[1,512,512]{2,1,0:T(8,128)(2,1)S(1)} all-gather(bf16[1,16,512]{2,1,0:T(8,128)(2,1)S(1)} %copy-done.4), channel_id=1, replica_groups=mesh['blk'=32,'req'=8] {'blk'}, dimensions={1}, use_global_device_ids=true | all-gather | bytes 540672 | tf_op jit(solution)/shard_map/all_gather | solution.py:113
  64.4 1.2 gather_fusion
  65.9 38.4 %all-gather = f32[512,2,4]{2,1,0:T(2,128)S(1)} all-gather(f32[16,2,4]{2,1,0:T(2,128)S(1)} %get-tuple-element.249), channel_id=2, replica_groups=mesh['blk'=32,'req'=8] {'blk'}, dimensions={0}, use_global_device_ids=true | all-gather | bytes 16896 | tf_op jit(solution)/shard_map/all_gather | solution.py:15
  104.6 39.6 %all-gather.1 = f32[512,2,4]{2,1,0:T(2,128)S(1)} all-gather(f32[16,2,4]{2,1,0:T(2,128)S(1)} %fusion.26), channel_id=3, replica_groups=mesh['blk'=32,'req'=8] {'blk'}, dimensions={0}, use_global_device_ids=true | all-gather | bytes 16896 | tf_op jit(solution)/shard_map/all_gather | solution.py:15
  144.3 1.1 copy.91
  145.4 1.1 copy.92
  146.8 1.5 copy.70
  149.1 1.4 reshape.386
  150.5 5.5 %all-to-all-start.1 = ((f32[32,1,128]{2,1,0:T(1,128)}), f32[32,1,128]{2,1,0:T(1,128)S(1)}, u32[]{:S(2)}, u32[]{:S(2)}) async-start(f32[32,1,128]{2,1,0:T(1,128)} %reshape.386), calls=%async_computation.1 | async-start | bytes 32768 | tf_op jit(solution)/shard_map/all_to_all | solution.py:122
  156.8 1.4 reshape.388
  158.2 4.9 %all-to-all-done.1 = f32[32,1,128]{2,1,0:T(1,128)S(1)} async-done(((f32[32,1,128]{2,1,0:T(1,128)}), f32[32,1,128]{2,1,0:T(1,128)S(1)}, u32[]{:S(2)}, u32[]{:S(2)}) %all-to-all-start.1) | async-done | bytes 16416 | tf_op jit(solution)/shard_map/all_to_all | solution.py:122
  163.1 6.7 %all-to-all-start.2 = ((f32[32,1,128]{2,1,0:T(1,128)}), f32[32,1,128]{2,1,0:T(1,128)S(1)}, u32[]{:S(2)}, u32[]{:S(2)}) async-start(f32[32,1,128]{2,1,0:T(1,128)} %reshape.388), calls=%async_computation.2 | async-start | bytes 32768 | tf_op jit(solution)/shard_map/all_to_all | solution.py:123
  170.5 2.6 copy.76
  175.8 1.0 all-to-all-done.2
  176.8 8.8 %all-to-all-start = ((f32[1,1,2,4,512,128]{5,3,2,1,0,4:T(4,128)}), f32[1,1,2,4,512,128]{5,3,2,1,0,4:T(4,128)S(1)}, u32[]{:S(2)}, u32[]{:S(2)}) async-start(f32[1,1,2,4,512,128]{5,3,2,1,0,4:T(4,128)} %copy.76), calls=%async_computation | async-start | bytes 4194304 | tf_op jit(solution)/shard_map/all_to_all | solution.py:124
  188.7 88.2 %while.19 = (s32[]{:T(128)}, f32[16,2,4,1]{0,2,3,1:T(4,128)S(1)}, f32[16,2,4,1]{0,2,3,1:T(4,128)S(1)}, f32[16,2,4,1,128]{4,3,2,1,0:T(1,128)S(1)}, f32[32,16,2,4,...) while((s32[]{:T(128)}, f32[16,2,4,1]{0,2,3,1:T(4,128)S(1)}, ...), condition=%wide.region_8.9_spmd, body=%wide.region_7.8_spmd.sunk | while | flops 50053 | bytes 337563 | solution.py:20
  190.1 0.9 constant_dynamic-slice_fusion.2
  192.9 0.9 constant_dynamic-slice_fusion.2
  195.8 0.9 constant_dynamic-slice_fusion.2
  198.6 0.9 constant_dynamic-slice_fusion.2
  204.3 0.9 constant_dynamic-slice_fusion.2
  210.0 0.9 constant_dynamic-slice_fusion.2
  215.7 0.9 constant_dynamic-slice_fusion.2
  227.2 0.9 constant_dynamic-slice_fusion.2
  230.0 0.9 constant_dynamic-slice_fusion.2
  249.9 0.9 constant_dynamic-slice_fusion.2
  277.4 29.2 %all_gather.39 = bf16[128,1024]{1,0:T(8,128)(2,1)S(1)} all-gather(bf16[16,1024]{1,0:T(8,128)(2,1)S(1)} %convert_element_type.51), channel_id=1, replica_groups=mesh['blk'=32,'req'=8] {'req'}, dimensions={0}, use_global_device_ids=true | all-gather | bytes 294912 | tf_op jit(solution)/shard_map/all_gather | solution.py:133
  308.2 28.9 %all_gather.32 = bf16[8,16,1024]{2,1,0:T(8,128)(2,1)S(1)} all-gather(bf16[1,16,1024]{2,1,0:T(8,128)(2,1)S(1)} %convert_element_type.46), channel_id=1, replica_groups=mesh['blk'=32,'req'=8] {'req'}, dimensions={0}, use_global_device_ids=true | all-gather | bytes 294912 | tf_op jit(solution)/shard_map/all_gather | solution.py:132
  (276 shorter events, 92.5 us)
Async XLA Ops:
  7.2 139.6 %all-gather.6.cloned.1.call-start = ((), (), s32[]{:S(2)}) async-start(), calls=%async_computation.3 | async-start | bytes 1081344 | tf_op jit(solution)/shard_map/all_gather | solution.py:114
  7.9 179.9 %all-gather.8.cloned.1.call-start = ((), (), s32[]{:S(2)}) async-start(), calls=%async_computation.4 | async-start | bytes 2162688 | tf_op jit(solution)/shard_map/all_gather | solution.py:15
  8.0 4.0 %copy-start.2 = (bf16[16,1024]{1,0:T(8,128)(2,1)S(1)}, bf16[16,1024]{1,0:T(8,128)(2,1)}, u32[]{:S(2)}) copy-start(bf16[16,1024]{1,0:T(8,128)(2,1)} %param.12) | copy-start | bytes 98308
  8.0 4.0 %copy-start.6 = (s32[16]{0:T(128)S(1)}, s32[16]{0:T(128)}, u32[]{:S(2)}) copy-start(s32[16]{0:T(128)} %param.18) | copy-start | bytes 196
  8.0 4.1 %copy-start.3 = (bf16[16,512]{1,0:T(8,128)(2,1)S(1)}, bf16[16,512]{1,0:T(8,128)(2,1)}, u32[]{:S(2)}) copy-start(bf16[16,512]{1,0:T(8,128)(2,1)} %param.14) | copy-start | bytes 49156
  16.5 3.3 copy-start.4
  16.5 49.1 %copy-start.1 = (bf16[1,128,512]{2,1,0:T(8,128)(2,1)S(1)}, bf16[1,128,512]{2,1,0:T(8,128)(2,1)}, u32[]{:S(2)}) copy-start(bf16[1,128,512]{2,1,0:T(8,128)(2,1)} %param.15) | copy-start | bytes 393220
  64.4 82.2 %copy-start.5 = (s32[136]{0:T(256)S(1)}, s32[136]{0:T(256)}, u32[]{:S(2)}) copy-start(s32[136]{0:T(256)} %param.19) | copy-start | bytes 1636
  65.7 82.6 %copy-start = (bf16[1,128,512]{2,1,0:T(8,128)(2,1)}, bf16[1,128,512]{2,1,0:T(8,128)(2,1)S(1)}, u32[]{:S(2)}) copy-start(bf16[1,128,512]{2,1,0:T(8,128)(2,1)S(1)} %bitcast_select_fusion.1) | copy-start | bytes 393220
  150.5 12.6 %all-to-all-start.1 = ((f32[32,1,128]{2,1,0:T(1,128)}), f32[32,1,128]{2,1,0:T(1,128)S(1)}, u32[]{:S(2)}, u32[]{:S(2)}) async-start(f32[32,1,128]{2,1,0:T(1,128)} %reshape.386), calls=%async_computation.1 | async-start | bytes 32768 | tf_op jit(solution)/shard_map/all_to_all | solution.py:122
  163.1 13.7 %all-to-all-start.2 = ((f32[32,1,128]{2,1,0:T(1,128)}), f32[32,1,128]{2,1,0:T(1,128)S(1)}, u32[]{:S(2)}, u32[]{:S(2)}) async-start(f32[32,1,128]{2,1,0:T(1,128)} %reshape.388), calls=%async_computation.2 | async-start | bytes 32768 | tf_op jit(solution)/shard_map/all_to_all | solution.py:123
  176.8 130.6 %all-to-all-start = ((f32[1,1,2,4,512,128]{5,3,2,1,0,4:T(4,128)}), f32[1,1,2,4,512,128]{5,3,2,1,0,4:T(4,128)S(1)}, u32[]{:S(2)}, u32[]{:S(2)}) async-start(f32[1,1,2,4,512,128]{5,3,2,1,0,4:T(4,128)} %copy.76), calls=%async_computation | async-start | bytes 4194304 | tf_op jit(solution)/shard_map/all_to_all | solution.py:124
Sparse Core Ops, SparseCore 0:
  10.8 79.0 all-gather.5
  92.7 76.8 all-gather.7
where the time goes:
time: 349 us; the launch traced here: 345 us
  blocking collectives  181 us (52%)
  other arithmetic  61.4 us (18%)
  local copies, waits for them, and re-layouts  55.1 us (16%)
  starting transfers between devices  21.1 us (6%)
  between operations  15 us (4%)
  waiting for transfers between devices  6.66 us (2%)
  matrix products  4.23 us (1%)
    all_gather x2, blocking collectives, merged(): gathered = jax.tree.map(lambda a: lax.all_gather(a, axis), part)  77.9 us
    all_gather x1, blocking collectives, per_device(): lax.all_gather(new_prefill, 'blk', axis=1, tiled=True)  44.6 us
    all_gather x1, blocking collectives, per_device(): lax.all_gather(decode_attn, 'req', axis=0, tiled=True)  29.2 us
    all_gather x1, blocking collectives, per_device(): lax.all_gather(prefill_attn, 'req', axis=0, tiled=True)  28.9 us
    dynamic_slice x36, local copies, waits for them, and re-layouts, take(): lax.dynamic_index_in_dim(a, source, 0, False)  27.4 us
    mul x31, other arithmetic, combine(): second_sum * second_scale[..., None]  21.9 us
    mul x31, other arithmetic, combine(): first_sum * first_scale[..., None] + second_sum * second_scale[..., None]  21.4 us
    add x31, other arithmetic, combine(): first_sum * first_scale[..., None] + second_sum * second_scale[..., None]  12 us
  transfers between devices with their start and end apart: 5, of which 2 were waited for; matrix products, arithmetic and copies ran while one was open for 34% of the time, Pallas kernels for 0%

commit v1 on v0

v1 whole, which is shorter than its diff:
```python
import functools
import math

import jax
import jax.numpy as jnp
from jax import lax
from jax.experimental import pallas as pl
from jax.experimental.pallas import tpu as pltpu
from jax.sharding import PartitionSpec as P

HEADS = 8
D = 128
TOK = 16
ROWS = 128
SLOTS = 16
NEG = -1e30
LOG2E = math.log2(math.e)
SCALE2 = D ** (-0.5) * LOG2E
BIG = 1 << 24
BF = jnp.bfloat16
F32 = jnp.float32
I32 = jnp.int32
NT = (((1,), (1,)), ((), ()))
TN = (((0,), (0,)), ((), ()))


def iota(shape, axis):
    return lax.broadcasted_iota(I32, shape, axis)


def dot(a, b, dims):
    return lax.dot_general(a, b, dims, preferred_element_type=F32)


def soft(s):
    m = jnp.max(s, axis=0, keepdims=True)
    p = jnp.exp2((s - m) * SCALE2)
    total = jnp.sum(p, axis=0, keepdims=True)
    return p, total, m * SCALE2 + jnp.log(total) * LOG2E


def put(ref, rows, o, lse):
    ref[0:rows, :] = o.astype(BF)
    hi = lse.astype(BF).astype(F32)
    mid = (lse - hi).astype(BF).astype(F32)
    low = lse - hi - mid
    row = iota((16, 128), 0)
    tile = jnp.where(row == 0, hi, jnp.where(row == 1, mid, jnp.where(row == 2, low, 0.0)))
    ref[rows : rows + 16, :] = tile.astype(BF)


def get_lse(ref, rows):
    return jnp.sum(ref[rows : rows + 16, :].astype(F32), axis=0, keepdims=True)


def merge(refs, rows):
    lses = [get_lse(ref, rows) for ref in refs]
    top = functools.reduce(jnp.maximum, lses)
    weights = [jnp.exp2(x - top) for x in lses]
    total = functools.reduce(jnp.add, weights)
    inv = 1.0 / total
    out = None
    for ref, w in zip(refs, weights):
        term = ref[0:rows, :].astype(F32) * (w * inv)
        out = term if out is None else out + term
    return out, top + jnp.log(total) * LOG2E


def body(
    Z, Y,
    q, dq, new, pc, dcache, off, lens, deal,
    pout, dout, cout,
    kbuf, vbuf, keyval, qall, dbuf, dsend, d1, d3, rdq, df,
    psend, pall, nk, nv, sel, nx, rsend, rall,
    s_load, s_loc,
    s_kv, r_kv, s_q, r_q, s_p, r_p, s_n, r_n,
    s_d1, r_d1, s_d3, r_d3, s_rd, r_rd, s_df, r_df, s_nx, r_nx, s_r, r_r,
):
    b = lax.axis_index("blk")
    r = lax.axis_index("req")
    c = lax.rem(b, 2)
    z = lax.rem(b // 2, Z)
    xh = b // (2 * Z)
    xl = lax.rem(r, 2)
    y = r // 2
    NP = 2 * Y

    def blk_at(dx, dz, dc):
        return lax.rem(xh + dx, 2) * (2 * Z) + lax.rem(z + dz, Z) * 2 + lax.rem(c + dc, 2)

    def req_at(dy, dl):
        return lax.rem(y + dy, Y) * 2 + lax.rem(xl + dl, 2)

    def rcopy(src, dst, ss, rs, blk, req):
        return pltpu.make_async_remote_copy(
            src_ref=src, dst_ref=dst, send_sem=ss, recv_sem=rs,
            device_id={"blk": blk, "req": req}, device_id_type=pl.DeviceIdType.MESH,
        )

    plane = [(0, 1), (1, 0), (1, 1)]
    reqs = [(dy, dl) for dy in range(Y) for dl in range(2)]

    loads = []
    for i in range(4):
        cp = pltpu.make_async_copy(
            dcache.at[pl.ds(4 * i, 4)], dbuf.at[pl.ds(4 * i, 4)], s_load.at[i]
        )
        cp.start()
        loads.append(cp)

    barrier = pltpu.get_barrier_semaphore()
    partners = [(blk_at(dx, 0, dc), r) for dx, dc in plane]
    partners += [(blk_at(0, k, dc), r) for k in range(1, Z) for dc in range(2)]
    partners += [(blk_at(0, 0, dc), req_at(dy, dl)) for dy, dl in reqs[1:] for dc in range(2)]
    for blk, req in partners:
        pl.semaphore_signal(
            barrier, inc=1, device_id={"blk": blk, "req": req},
            device_id_type=pl.DeviceIdType.MESH,
        )

    lane = iota((1, 128), 1)
    lane_slot = lax.rem(lane, SLOTS)
    zero = jnp.zeros((SLOTS, D), BF)
    rows = []
    for h in range(HEADS):
        x = dq[:, h * D : (h + 1) * D]
        rows.append(jnp.concatenate([x, zero] if h < 4 else [zero, x], axis=1))
    qbd = jnp.concatenate(rows, axis=0)
    limit = jnp.zeros((1, 128), I32)
    for j in range(SLOTS):
        limit = jnp.where(lane_slot == j, lens[j], limit)
    sc = jnp.zeros((ROWS, 128), F32)
    for i in range(4):
        loads[i].wait()
        keys = dbuf[4 * i : 4 * i + 4, :, 0 : 2 * D].reshape(4 * ROWS, 2 * D)
        s = dot(keys, qbd, NT)
        for j in range(4):
            sc = jnp.where(lane_slot == 4 * i + j, s[j * ROWS : (j + 1) * ROWS], sc)
    pos = b * ROWS + iota((ROWS, 128), 0)
    p, total, lse = soft(jnp.where(pos <= limit, sc, NEG))
    p_t = jnp.transpose(p)
    row_slot = lax.rem(iota((128, 128), 0), SLOTS)
    p_all = jnp.concatenate(
        [jnp.where(row_slot == j, p_t, 0.0).astype(BF) for j in range(SLOTS)], axis=1
    )
    values = dbuf[:, :, 2 * D : 4 * D].reshape(SLOTS * ROWS, 2 * D)
    o = jnp.dot(p_all, values, preferred_element_type=F32)
    o = jnp.concatenate([o[0:64, 0:D], o[64:128, D : 2 * D]], axis=0)
    o_t = jnp.transpose(o) * (1.0 / total)
    for i in range(4):
        put(dsend.at[i], 32, o_t[32 * i : 32 * i + 32], lse)

    pl.semaphore_wait(barrier, len(partners))

    kv_copies = []
    for i, (dx, dc) in enumerate(plane):
        j = 2 * dx + dc
        h = lax.rem(c + dc, 2)
        kcol = pl.multiple_of(h * D, D)
        vcol = pl.multiple_of(2 * D + h * D, D)
        blk = blk_at(dx, 0, dc)
        for n, (src, dst) in enumerate([
            (pc.at[:, pl.ds(kcol, D)], kbuf.at[pl.ds(j * ROWS, ROWS)]),
            (pc.at[:, pl.ds(vcol, D)], vbuf.at[pl.ds(j * ROWS, ROWS)]),
            (new.at[:, pl.ds(kcol, D)], kbuf.at[pl.ds(4 * ROWS + j * TOK, TOK)]),
            (new.at[:, pl.ds(vcol, D)], vbuf.at[pl.ds(4 * ROWS + j * TOK, TOK)]),
        ]):
            cp = rcopy(src, dst, s_kv.at[4 * i + n], r_kv.at[4 * i + n], blk, r)
            cp.start()
            kv_copies.append(cp)
    q_copies = {}
    order = []
    for k in range(1, Z // 2 + 1):
        order.append(k)
        if Z - k != k:
            order.append(Z - k)
    for k in order + [0]:
        for dc in range(2):
            if k == 0 and dc == 0:
                continue
            half = pl.multiple_of(lax.rem(c + dc, 2) * 4 * D, 4 * D)
            cp = rcopy(
                q.at[:, pl.ds(half, 4 * D)], qall.at[k, dc],
                s_q.at[2 * k + dc], r_q.at[2 * k + dc], blk_at(0, k, dc), r,
            )
            cp.start()
            q_copies[k, dc] = cp
    my_plane = xh * 2 + c
    d1_copies = []
    for i, (dx, dc) in enumerate(plane):
        to = lax.rem(xh + dx, 2) * 2 + lax.rem(c + dc, 2)
        cp = rcopy(dsend.at[to], d1.at[i], s_d1.at[i], r_d1.at[i], blk_at(dx, 0, dc), r)
        cp.start()
        d1_copies.append(cp)

    kcol = pl.multiple_of(c * D, D)
    vcol = pl.multiple_of(2 * D + c * D, D)
    half = pl.multiple_of(c * 4 * D, 4 * D)
    own = []
    for n, (src, dst) in enumerate([
        (pc.at[:, pl.ds(kcol, D)], kbuf.at[pl.ds(0, ROWS)]),
        (pc.at[:, pl.ds(vcol, D)], vbuf.at[pl.ds(0, ROWS)]),
        (new.at[:, pl.ds(kcol, D)], kbuf.at[pl.ds(4 * ROWS, TOK)]),
        (new.at[:, pl.ds(vcol, D)], vbuf.at[pl.ds(4 * ROWS, TOK)]),
        (q.at[:, pl.ds(half, 4 * D)], qall.at[0, 0]),
    ]):
        cp = pltpu.make_async_copy(src, dst, s_loc.at[n])
        cp.start()
        own.append(cp)

    offset = off[0]
    for j in range(4):
        blk = blk_at(j // 2, 0, j % 2)
        at = blk * ROWS + iota((ROWS, 128), 0)
        keyval[j * ROWS : (j + 1) * ROWS, :] = jnp.where(at < offset, at, BIG)
        keyval[4 * ROWS + j * TOK : 4 * ROWS + (j + 1) * TOK, :] = (
            offset + blk * TOK + iota((TOK, 128), 0)
        )

    for cp in d1_copies:
        cp.wait_recv()
    part, lse = merge([dsend.at[my_plane]] + [d1.at[i] for i in range(3)], 32)
    put(d3.at[0], 32, part, lse)
    d3_copies = []
    for k in order:
        cp = rcopy(d3.at[0], d3.at[k], s_d3.at[k], r_d3.at[k], blk_at(0, k, 0), r)
        cp.start()
        d3_copies.append(cp)

    for cp in own:
        cp.wait()
    for cp in kv_copies:
        cp.wait_recv()
    v_t = jnp.transpose(vbuf[...].astype(F32)).astype(BF)
    lane_core = lax.rem(lane // TOK, 2)
    lane_tok = lax.rem(lane, TOK)
    p_copies = {}
    for k in order + [0]:
        for dc in range(2):
            if (k, dc) in q_copies:
                q_copies[k, dc].wait_recv()
        qrows = jnp.concatenate(
            [qall[k, dc, :, h * D : (h + 1) * D] for h in range(4) for dc in range(2)], axis=0
        )
        s = dot(kbuf[...], qrows, NT)
        home = xh * (2 * Z) + lax.rem(z + Z - k, Z) * 2
        tok = (home + lax.rem(c + lane_core, 2)) * TOK + lane_tok
        p, total, lse = soft(jnp.where(keyval[...] <= offset + tok, s, NEG))
        o_t = jnp.dot(v_t, p.astype(BF), preferred_element_type=F32)
        if k == 0:
            put(pall.at[0], D, o_t * (1.0 / total), lse)
        else:
            put(psend.at[k], D, o_t * (1.0 / total), lse)
            cp = rcopy(psend.at[k], pall.at[k], s_p.at[k], r_p.at[k], blk_at(0, Z - k, 0), r)
            cp.start()
            p_copies[k] = cp

    n_copies = []
    for k in order:
        for n, (src, dst) in enumerate([
            (kbuf.at[pl.ds(4 * ROWS, 4 * TOK)], nk.at[pl.ds(k * 4 * TOK, 4 * TOK)]),
            (vbuf.at[pl.ds(4 * ROWS, 4 * TOK)], nv.at[pl.ds(k * 4 * TOK, 4 * TOK)]),
        ]):
            cp = rcopy(src, dst, s_n.at[2 * k + n], r_n.at[2 * k + n], blk_at(0, k, 0), r)
            cp.start()
            n_copies.append(cp)
    nk[0 : 4 * TOK, :] = kbuf[4 * ROWS : 4 * ROWS + 4 * TOK, :]
    nv[0 : 4 * TOK, :] = vbuf[4 * ROWS : 4 * ROWS + 4 * TOK, :]

    for cp in d3_copies:
        cp.wait_recv()
    part, lse = merge([d3.at[k] for k in range(Z)], 32)
    rdq[0] = part.astype(BF)
    rd_copies = []
    for i, (dy, dl) in enumerate(reqs):
        if i:
            cp = rcopy(rdq.at[0], rdq.at[i], s_rd.at[i], r_rd.at[i], b, req_at(dy, dl))
            cp.start()
            rd_copies.append(cp)

    for k in order:
        p_copies[k].wait_recv()
    part, lse = merge([pall.at[k] for k in range(Z)], D)
    att = jnp.transpose(part).astype(BF)
    for dc in range(2):
        for h in range(4):
            lo = h * 2 * TOK + dc * TOK
            rsend[dc, :, h * D : (h + 1) * D] = att[lo : lo + TOK, :]
    r_copies = []
    for i, (dy, dl) in enumerate(reqs):
        for dc in range(2):
            if i or dc:
                cp = rcopy(
                    rsend.at[dc], rall.at[i, dc], s_r.at[2 * i + dc], r_r.at[2 * i + dc],
                    blk_at(0, 0, dc), req_at(dy, dl),
                )
                cp.start()
                r_copies.append(cp)

    for cp in rd_copies:
        cp.wait_recv()
    target = r * SLOTS + lax.rem(iota((128, 128), 0), SLOTS)
    same_head = iota((128, 128), 0) // SLOTS == iota((128, 128), 1) // SLOTS
    picked = jnp.zeros((32, 128), F32)
    for i, (dy, dl) in enumerate(reqs):
        source = req_at(Y - dy, dl)
        dealt = jnp.zeros((1, 128), I32)
        for j in range(SLOTS):
            dealt = jnp.where(lane_slot == j, deal[NP + source * SLOTS + j], dealt)
        chosen = jnp.where(same_head & (target == dealt), 1.0, 0.0).astype(BF)
        picked = picked + dot(rdq[i], chosen, NT)
    df[my_plane] = picked.astype(BF)
    df_copies = []
    for i, (dx, dc) in enumerate(plane):
        cp = rcopy(
            df.at[my_plane], df.at[my_plane], s_df.at[i], r_df.at[i], blk_at(dx, 0, dc), r
        )
        cp.start()
        df_copies.append(cp)

    for cp in n_copies:
        cp.wait_recv()
    width = Z * 4 * TOK
    col = iota((1, width), 1)
    ck = col // (4 * TOK)
    cj = lax.rem(col // TOK, 4)
    cblk = (
        lax.rem(xh + cj // 2, 2) * (2 * Z)
        + lax.rem(z + Z - ck, Z) * 2
        + lax.rem(c + lax.rem(cj, 2), 2)
    )
    tok_of = offset + cblk * TOK + lax.rem(col, TOK)
    partner = blk_at(0, 0, 1)
    picks = []
    for blk in (b, partner):
        hot = jnp.where(blk * ROWS + iota((ROWS, width), 0) == tok_of, 1.0, 0.0).astype(BF)
        picks.append((
            jnp.dot(hot, nk[...], preferred_element_type=F32).astype(BF),
            jnp.dot(hot, nv[...], preferred_element_type=F32).astype(BF),
        ))
    sel[0] = picks[1][0]
    sel[1] = picks[1][1]
    nx_copy = rcopy(sel, nx, s_nx.at[0], r_nx.at[0], partner, r)
    nx_copy.start()

    for cp in r_copies:
        cp.wait_recv()
    for dc in range(2):
        acc = rsend[0] if dc == 0 else rall[0, 1]
        for i, (dy, dl) in enumerate(reqs):
            if i:
                acc = jnp.where(deal[req_at(Y - dy, dl)] == r, rall[i, dc], acc)
        half = pl.multiple_of(lax.rem(c + dc, 2) * 4 * D, 4 * D)
        pout[:, pl.ds(half, 4 * D)] = acc
    for cp in df_copies:
        cp.wait_recv()
    full = jnp.transpose(df[...].reshape(128, 128).astype(F32)).astype(BF)
    for h in range(HEADS):
        dout[:, h * D : (h + 1) * D] = full[h * SLOTS : (h + 1) * SLOTS, :]
    nx_copy.wait_recv()
    at = b * ROWS + iota((ROWS, D), 0)
    inside = (at >= offset) & (at < offset + 2 * 2 * Z * TOK)
    for n in range(2):
        own_col = pl.multiple_of(2 * n * D + c * D, D)
        other_col = pl.multiple_of(2 * n * D + lax.rem(c + 1, 2) * D, D)
        cout[:, pl.ds(own_col, D)] = jnp.where(inside, picks[0][n], pc[:, pl.ds(own_col, D)])
        cout[:, pl.ds(other_col, D)] = jnp.where(inside, nx[n], pc[:, pl.ds(other_col, D)])

    for group in (
        kv_copies, list(q_copies.values()), d1_copies, d3_copies, list(p_copies.values()),
        n_copies, rd_copies, r_copies, df_copies, [nx_copy],
    ):
        for cp in group:
            cp.wait_send()


def make_kernel(Z, Y):
    NR = 2 * Y
    vm = pl.BlockSpec(memory_space=pltpu.VMEM)
    sm = pl.BlockSpec(memory_space=pltpu.SMEM)
    dma = lambda n: pltpu.SemaphoreType.DMA((n,))
    scratch = [
        pltpu.VMEM((4 * ROWS + 4 * TOK, D), BF),
        pltpu.VMEM((4 * ROWS + 4 * TOK, D), BF),
        pltpu.VMEM((4 * ROWS + 4 * TOK, 128), I32),
        pltpu.VMEM((Z, 2, TOK, 4 * D), BF),
        pltpu.VMEM((SLOTS, ROWS, 4 * D), BF),
        pltpu.VMEM((4, 48, 128), BF),
        pltpu.VMEM((3, 48, 128), BF),
        pltpu.VMEM((Z, 48, 128), BF),
        pltpu.VMEM((NR, 32, 128), BF),
        pltpu.VMEM((4, 32, 128), BF),
        pltpu.VMEM((Z, 144, 128), BF),
        pltpu.VMEM((Z, 144, 128), BF),
        pltpu.VMEM((Z * 4 * TOK, D), BF),
        pltpu.VMEM((Z * 4 * TOK, D), BF),
        pltpu.VMEM((2, ROWS, D), BF),
        pltpu.VMEM((2, ROWS, D), BF),
        pltpu.VMEM((2, TOK, 4 * D), BF),
        pltpu.VMEM((NR, 2, TOK, 4 * D), BF),
        dma(4), dma(5),
        dma(12), dma(12), dma(2 * Z), dma(2 * Z), dma(Z), dma(Z), dma(2 * Z), dma(2 * Z),
        dma(3), dma(3), dma(Z), dma(Z), dma(NR), dma(NR), dma(3), dma(3), dma(1), dma(1),
        dma(2 * NR), dma(2 * NR),
    ]
    return pl.pallas_call(
        functools.partial(body, Z, Y),
        out_shape=(
            jax.ShapeDtypeStruct((TOK, HEADS * D), BF),
            jax.ShapeDtypeStruct((SLOTS, HEADS * D), BF),
            jax.ShapeDtypeStruct((ROWS, 4 * D), BF),
        ),
        in_specs=[vm, vm, vm, vm, pl.BlockSpec(memory_space=pl.ANY), sm, sm, sm],
        out_specs=(vm, vm, vm),
        scratch_shapes=scratch,
        compiler_params=pltpu.CompilerParams(
            collective_id=0, has_side_effects=True, vmem_limit_bytes=48 * 1024 * 1024
        ),
    )


def per_device(
    Z, Y, prefill_queries, decode_queries, new_prefill, new_decode, prefill_cache, decode_cache,
    prefill_offsets, decode_lengths, dealing,
):
    positions = lax.axis_index("blk") * ROWS + jnp.arange(ROWS, dtype=I32)
    written = positions[None, :] == decode_lengths[:, None]
    decode_cache_out = jnp.where(written[:, :, None], new_decode[:, None, :], decode_cache)
    prefill_out, decode_out, prefill_cache_out = make_kernel(Z, Y)(
        prefill_queries[0], decode_queries, new_prefill[0], prefill_cache[0], decode_cache_out,
        prefill_offsets, decode_lengths, dealing,
    )
    return prefill_out[None], decode_out, prefill_cache_out[None], decode_cache_out


def solution(mesh):
    Z, Y = mesh.shape["blk"] // 4, mesh.shape["req"] // 2
    in_specs = (
        P("req", "blk", None), P("req", None), P("req", "blk", None), P("req", None),
        P("req", "blk", None), P("req", "blk", None), P("req"), P("req"), P(),
    )
    out_specs = (
        P("req", "blk", None), P("req", None), P("req", "blk", None), P("req", "blk", None),
    )
    return jax.shard_map(
        functools.partial(per_device, Z, Y), mesh=mesh, in_specs=in_specs, out_specs=out_specs,
        check_vma=False,
    )
```

time: 349 us -> 44.5 us (0.13)
  the two profiles are of different devices: /device:TPU:6 before, /device:TPU:1 now
where the time goes in v1:
time: 44.5 us; the launch traced here: 44.4 us
  Pallas kernels  38.5 us (87%)
  other arithmetic  2.61 us (6%)
  local copies, waits for them, and re-layouts  1.93 us (4%)
  between operations  1.4 us (3%)
    pallas_call x1, Pallas kernels, per_device(): make_kernel(Z, Y)  38.5 us
    unnamed x17, local copies, waits for them, and re-layouts  1.93 us
    select_n x1, other arithmetic, per_device(): jnp.where(written[:, :, None], new_decode[:, None, :], decode_cache)  1.88 us

profile of v1, /device:TPU:1, one launch (start us, length us, event | category | flops | bytes accessed | tf_op | source)
XLA Modules:
  0.0 44.4 jit_solution(10212763903926784953)
XLA Ops:
  1.3 0.7 %broadcast_compare_fusion = pred[16,128]{1,0:T(8,128)(4,1)S(1)} fusion(s32[128]{0:T(128)S(1)} %iota_add_fusion, s32[16]{0:T(128)} %lens.1), kind=kLoop, calls=%fused_computation.1 | loop fusion | flops 2048 | bytes 2624 | tf_op jit(solution)/shard_map/eq | solution.py:427
  2.0 0.0 copy-start.1
  2.0 0.0 copy-start.2
  2.0 0.0 copy-start.3
  2.0 0.0 copy-start.4
  2.1 0.0 copy-start.5
  2.1 0.0 copy-start.6
  2.1 1.9 %broadcast_select_fusion.dcache = bf16[16,128,512]{2,1,0:T(8,128)(2,1)S(1)} fusion(bf16[16,128,512]{2,1,0:T(8,128)(2,1)} %param.14, pred[16,128]{1,0:T(8,128)(4,1)S(1)} %broadcast_compare_fusion, bf16[16,512]{1,0:T(8,128)(2,1)} %param.12), kind=kLoop, calls=%fused_computation | loop fusion | flops 1048576 | bytes 4212736 | tf_op jit(solution)/shard_map/jit(_where)/select_n | solution.py:428
  4.0 0.0 copy-done.1
  4.0 0.0 copy-done.2
  4.0 0.0 copy-done.3
  4.0 0.0 copy-done.4
  4.0 0.0 copy-done.5
  4.0 0.0 copy-done.6
  4.0 0.0 copy-start
  4.0 38.5 %shard_map.120 = (bf16[16,1024]{1,0:T(8,128)(2,1)S(1)}, bf16[16,1024]{1,0:T(8,128)(2,1)S(1)}, bf16[128,512]{1,0:T(8,128)(2,1)S(1)}) custom-call(bf16[16,1024]{1,0:T(8,128)(2,1)S(1)} %bitcast.7, bf16[16,1024]{1,0:T(8,128)(2,1)S(1)} %copy-done.3, bf16[16,512]{1,0:T(8,128)(2,1)S(1)} %bitcast.9, bf16[128,512]{1,0:T(8,128)(2,1)S(1)} %bitcast.6, ...), custom_call_target="tpu_custom_call" | custom-call | tf_op jit(solution)/shard_map/pallas_call | solution.py:429
  42.5 0.6 %copy.17 = bf16[1,16,1024]{2,1,0:T(8,128)(2,1)} copy(bf16[1,16,1024]{2,1,0:T(8,128)(2,1)S(1)} %bitcast.8) | data formatting | bytes 65536
  43.1 0.6 %copy.18 = bf16[16,1024]{1,0:T(8,128)(2,1)} copy(bf16[16,1024]{1,0:T(8,128)(2,1)S(1)} %get-tuple-element.15) | data formatting | bytes 65536
  43.8 0.7 %copy.19 = bf16[1,128,512]{2,1,0:T(8,128)(2,1)} copy(bf16[1,128,512]{2,1,0:T(8,128)(2,1)S(1)} %bitcast.5) | data formatting | bytes 262144
  44.4 0.0 copy-done
  (1 shorter events, 0.0 us)
Async XLA Ops:
  2.0 1.9 %copy-start.1 = (bf16[1,128,512]{2,1,0:T(8,128)(2,1)S(1)}, bf16[1,128,512]{2,1,0:T(8,128)(2,1)}, u32[]{:S(2)}) copy-start(bf16[1,128,512]{2,1,0:T(8,128)(2,1)} %param.13) | copy-start | bytes 393220
  2.0 1.9 %copy-start.2 = (bf16[1,16,1024]{2,1,0:T(8,128)(2,1)S(1)}, bf16[1,16,1024]{2,1,0:T(8,128)(2,1)}, u32[]{:S(2)}) copy-start(bf16[1,16,1024]{2,1,0:T(8,128)(2,1)} %param.9) | copy-start | bytes 98308
  2.0 2.0 %copy-start.3 = (bf16[16,1024]{1,0:T(8,128)(2,1)S(1)}, bf16[16,1024]{1,0:T(8,128)(2,1)}, u32[]{:S(2)}) copy-start(bf16[16,1024]{1,0:T(8,128)(2,1)} %dq.1) | copy-start | bytes 98308
  2.0 2.0 %copy-start.4 = (bf16[1,16,512]{2,1,0:T(8,128)(2,1)S(1)}, bf16[1,16,512]{2,1,0:T(8,128)(2,1)}, u32[]{:S(2)}) copy-start(bf16[1,16,512]{2,1,0:T(8,128)(2,1)} %param.11) | copy-start | bytes 49156
  2.1 2.0 %copy-start.5 = (s32[16]{0:T(128)S(1)}, s32[16]{0:T(128)}, u32[]{:S(2)}) copy-start(s32[16]{0:T(128)} %lens.1) | copy-start | bytes 196
  2.1 1.9 %copy-start.6 = (s32[136]{0:T(256)S(1)}, s32[136]{0:T(256)}, u32[]{:S(2)}) copy-start(s32[136]{0:T(256)} %deal.1) | copy-start | bytes 1636
  4.0 40.4 %copy-start = (bf16[16,128,512]{2,1,0:T(8,128)(2,1)}, bf16[16,128,512]{2,1,0:T(8,128)(2,1)S(1)}, u32[]{:S(2)}) copy-start(bf16[16,128,512]{2,1,0:T(8,128)(2,1)S(1)} %broadcast_select_fusion.dcache) | copy-start | bytes 6291460
